TPU v7x, 128 devices: a whole 4x4x4 slice. The times are simulated.
128 devices in a mesh: tm: 4 (over x), op: 32 (over y, z, core).
Axes of the slice: x: 4, y: 4, z: 4, core: 2. Of those that a mesh axis runs over, the one named last changes fastest.
Arguments:
- sink_elem: bfloat16 [2, 4, 2048, 16384], P(None, 'tm', 'op'), may hold values from -6 to 6
- source_elem: bfloat16 [2, 2, 2048, 16384], P(None, None, None, 'op'), may hold values from -6 to 6
- peram: bfloat16 [2, 4, 2, 512, 512], P(None, 'tm', None, 'op'), may hold values from -4 to 4
- pair_list: int32 [16, 1], replicated, may hold values from 0 to 15
- spin_sets: int32 [16, 3], replicated, may hold values from 0 to 3
Outputs:
- correlator: float32 [2, 4, 2, 16, 1], P(None, 'tm')
All inputs are finite; a program needn't handle non-finite values.
Results may differ from a plain program's by a relative error of at most 0.0041.
Values may be sent and summed in bfloat16 or wider, within the bound.
A program may use at most 192 MiB of HBM per device.

v0:
```python
import jax
import jax.numpy as jnp
from jax import lax
from jax.sharding import PartitionSpec as P

NEV = 128
NSPIN = 4
NOP = 16
TSRC = 2
PAIRS = 1


def complex_matrix(block):
    upper = jnp.concatenate([block[0], block[1]], axis=1)
    lower = jnp.concatenate([-block[1], block[0]], axis=1)
    return jnp.stack([upper, lower])


def on_device(sink_elem, source_elem, peram, pair_list, spin_sets):
    tau_all = lax.all_gather(peram, "op", axis=3, tiled=True)
    position = lax.axis_index("op")
    rows = sink_elem.shape[2]
    local_times = sink_elem.shape[1]
    span = min(rows, NEV)
    cols = source_elem.shape[3]

    def spin_block(local, t0, left, right):
        return lax.dynamic_slice(tau_all[:, local, t0], (0, left * NEV, right * NEV), (2, NEV, NEV))

    def sink_side(local, t0, p):
        op_now = (position * rows + 0) // NEV
        mine = spin_sets[op_now]
        theirs = spin_sets[pair_list[op_now, p]]
        third = complex_matrix(spin_block(local, t0, mine[2], theirs[2]))
        second = complex_matrix(spin_block(local, t0, mine[1], theirs[1]))
        phi = sink_elem[:, local, 0:span].reshape(2, span * NEV, NEV)
        x_both = jnp.einsum("cxk,ckb->xb", phi, third, preferred_element_type=jnp.float32)
        x_both = x_both.astype(jnp.bfloat16).reshape(span, NEV, 2, NEV)
        y_both = jnp.einsum("ijck,cjb->ibk", x_both, second, preferred_element_type=jnp.float32)
        y_both = y_both.astype(jnp.bfloat16).reshape(span, 2, NEV * NEV)
        pieces = jnp.transpose(y_both, (1, 0, 2))
        return pieces

    partial_terms = {}
    combos = [
        (local, t0, p) for local in range(local_times) for t0 in range(TSRC) for p in range(PAIRS)
    ]
    stacked = jnp.stack([sink_side(local, t0, p) for local, t0, p in combos], axis=1)
    columns = lax.all_to_all(stacked, "op", split_axis=3, concat_axis=2, tiled=True)
    for index, combo in enumerate(combos):
        column_t0 = combo[1]
        other = pair_list[:, combo[2]]
        source = source_elem[:, column_t0].reshape(2, NOP, NEV, cols)
        chosen = jnp.take(source, other, axis=1)
        tiles = columns[:, index].reshape(2, NOP, NEV, cols)

        def inner(a, b):
            return jnp.einsum("oic,ojc->oij", a, b, preferred_element_type=jnp.float32)

        m_re = inner(tiles[0], chosen[0]) + inner(tiles[1], chosen[1])
        m_im = inner(tiles[1], chosen[0]) - inner(tiles[0], chosen[1])
        blocks = tau_all[:, combo[0], column_t0].reshape(2, NSPIN, NEV, NSPIN, NEV)
        blocks = jnp.transpose(blocks, (1, 3, 0, 2, 4))
        first = blocks[spin_sets[:, 0], spin_sets[other, 0]].astype(jnp.float32)
        c_re = jnp.sum(first[:, 0] * m_re - first[:, 1] * m_im, axis=(1, 2))
        c_im = jnp.sum(first[:, 0] * m_im + first[:, 1] * m_re, axis=(1, 2))
        partial_terms[combo] = jnp.stack([c_re, c_im])
    local = 0
    per_time = []
    for t0 in range(TSRC):
        per_time.append(jnp.stack([partial_terms[local, t0, 0]], axis=-1))
    per_local = [jnp.stack(per_time, axis=1)]
    partial_sum = jnp.stack(per_local, axis=1)
    totals = lax.psum(partial_sum, "op")
    return totals * (1.0 / float(NEV**3))


def solution(mesh):
    in_specs = (
        P(None, "tm", "op", None),
        P(None, None, None, "op"),
        P(None, "tm", None, "op", None),
        P(),
        P(),
    )
    out_specs = P(None, "tm", None, None, None)
    return jax.shard_map(
        on_device, mesh=mesh, in_specs=in_specs, out_specs=out_specs, check_vma=False
    )
```

profile of v0, /device:TPU:1, one launch (start us, length us, event | category | flops | bytes accessed | tf_op | source)
XLA Modules:
  0.0 462.1 jit_solution(5356037397111504323)
XLA Ops:
  6.5 1.5 copy.40
  8.1 1.2 constant_dynamic-slice_fusion.1
  11.3 0.8 constant_dynamic-slice_fusion
  15.2 7.4 %reshape_squeeze.19 = bf16[2,8192,128]{2,1,0:T(8,128)(2,1)} reshape(bf16[2,1,64,16384]{3,2,1,0:T(8,128)(2,1)} %param.7) | data formatting | bytes 8388608 | tf_op jit(solution)/shard_map/reshape;squeeze | solution.py:36
  22.6 34.7 %all-gather.2.cloned.1.call-done = bf16[2,1,2,512,512]{4,2,1,0,3:T(2,128)(2,1)} async-done(((bf16[2,1,2,16,512]{4,2,1,0,3:T(2,128)(2,1)}), bf16[2,1,2,512,512]{4,2,1,0,3:T(2,128)(2,1)}) %all-gather.2.cloned.1.call-update) | async-done | bytes 2097168 | tf_op jit(solution)/shard_map/all_gather | solution.py:20
  57.3 6.5 %fusion.57 = (bf16[2,1,1,512,512]{4,2,1,0,3:T(2,128)(2,1)}, bf16[2,1,1,512,512]{4,2,1,0,3:T(2,128)(2,1)S(1)}) fusion(bf16[2,1,2,512,512]{4,2,1,0,3:T(2,128)(2,1)} %all-gather.2.cloned.1.call-done), kind=kLoop, calls=%fused_computation.113 | loop fusion | bytes 4194304 | tf_op jit(solution)/shard_map/slice | solution.py:62
  63.8 4.6 copy.59
  68.4 4.2 copy.60
  72.6 0.8 dynamic-slice_bitcast_fusion.3
  73.4 0.8 fusion.53
  74.2 3.5 fusion.15
  77.7 1.2 copy.61
  78.9 7.4 %fusion.2 = bf16[64,256,128]{2,1,0:T(8,128)(2,1)} fusion(bf16[64,128,2,128]{1,0,3,2:T(8,128)(2,1)S(1)} %bitcast.218, bf16[1,128,256]{1,2,0:T(8,128)(2,1)S(1)} %get-tuple-element.35, bf16[1,128,256]{1,2,0:T(8,128)(2,1)S(1)} %get-tuple-element.34), kind=kOutput, calls=%fused_computation.12 | convolution fusion | flops 1076101120 | bytes 8519680 | tf_op jit(solution)/shard_map/ijck,cjb->ibk/dot_general | solution.py:39
  86.4 6.9 %reshape.75 = bf16[64,2,16384]{2,1,0:T(2,128)(2,1)} reshape(bf16[64,256,128]{2,1,0:T(8,128)(2,1)} %fusion.2) | data formatting | bytes 8388608 | tf_op jit(solution)/shard_map/reshape | solution.py:40
  93.2 6.6 %copy.83 = bf16[64,2,16384]{2,0,1:T(8,128)(2,1)} copy(bf16[64,2,16384]{2,1,0:T(2,128)(2,1)} %reshape.75) | data formatting | bytes 8388608 | tf_op jit(solution)/shard_map/reshape | solution.py:40
  99.9 1.3 fusion.14
  101.2 1.2 copy.62
  102.4 7.4 %fusion.3 = bf16[64,256,128]{2,1,0:T(8,128)(2,1)} fusion(bf16[64,128,2,128]{1,0,3,2:T(8,128)(2,1)S(1)} %bitcast.219, bf16[1,128,256]{1,2,0:T(8,128)(2,1)S(1)} %get-tuple-element.39, bf16[1,128,256]{1,2,0:T(8,128)(2,1)S(1)} %get-tuple-element.38), kind=kOutput, calls=%fused_computation.13 | convolution fusion | flops 1076101120 | bytes 8519680 | tf_op jit(solution)/shard_map/ijck,cjb->ibk/dot_general | solution.py:39
  109.8 6.9 %reshape.77 = bf16[64,2,16384]{2,1,0:T(2,128)(2,1)} reshape(bf16[64,256,128]{2,1,0:T(8,128)(2,1)} %fusion.3) | data formatting | bytes 8388608 | tf_op jit(solution)/shard_map/reshape | solution.py:40
  116.7 6.6 %copy.82 = bf16[64,2,16384]{2,0,1:T(8,128)(2,1)} copy(bf16[64,2,16384]{2,1,0:T(2,128)(2,1)} %reshape.77) | data formatting | bytes 8388608 | tf_op jit(solution)/shard_map/reshape | solution.py:40
  123.3 6.2 %pad_maximum_fusion = bf16[2,2,64,16384]{3,2,1,0:T(8,128)(2,1)} fusion(bf16[2,1,64,16384]{3,2,1,0:T(8,128)(2,1)} %bitcast.222, bf16[2,1,64,16384]{3,2,1,0:T(8,128)(2,1)S(1)} %bitcast.220), kind=kLoop, calls=%fused_computation.9 | loop fusion | flops 4194304 | bytes 16777216 | tf_op jit(solution)/shard_map/stack | solution.py:48
  129.5 34.5 %copy.49 = bf16[2,2,64,16384]{2,1,0,3:T(2,128)(2,1)} copy(bf16[2,2,64,16384]{3,2,1,0:T(8,128)(2,1)} %pad_maximum_fusion) | data formatting | bytes 16777216 | tf_op jit(solution)/shard_map/stack | solution.py:48
  164.0 26.7 %reshape.124 = bf16[32,2,65536]{2,1,0:T(2,128)(2,1)} reshape(bf16[16384,2,2,64]{3,2,1,0:T(2,128)(2,1)} %bitcast.211) | data formatting | bytes 16777216
  190.7 5.4 %all-to-all-start = ((bf16[32,2,65536]{2,1,0:T(2,128)(2,1)}), bf16[32,2,65536]{2,1,0:T(2,128)(2,1)}, u32[]{:S(2)}, u32[]{:S(2)}) async-start(bf16[32,2,65536]{2,1,0:T(2,128)(2,1)} %reshape.124), calls=%async_computation | async-start | bytes 16777216 | tf_op jit(solution)/shard_map/all_to_all | solution.py:49
  196.2 5.8 %fusion.56 = (bf16[2,1,2048,512]{3,2,1,0:T(8,128)(2,1)}, bf16[2,1,2048,512]{3,2,1,0:T(8,128)(2,1)}) fusion(bf16[2,2,2048,512]{3,2,1,0:T(8,128)(2,1)} %param.8), kind=kLoop, calls=%fused_computation.112 | loop fusion | bytes 16777216 | tf_op jit(solution)/shard_map/slice | solution.py:53
  202.0 5.0 %gather_fusion.3 = bf16[16,2,128,512]{3,2,1,0:T(8,128)(2,1)} fusion(bf16[2,16,128,512]{3,2,1,0:T(8,128)(2,1)} %bitcast.223, s32[1024]{0:T(1024)S(1)} %pad_clamp_fusion), kind=kCustom, calls=%fused_computation.clone | custom fusion | bytes 8388672 | tf_op jit(solution)/shard_map/jit(_take)/gather | solution.py:54
  207.0 5.0 %gather_fusion.4 = bf16[16,2,128,512]{3,2,1,0:T(8,128)(2,1)} fusion(bf16[2,16,128,512]{3,2,1,0:T(8,128)(2,1)} %bitcast.221, s32[1024]{0:T(1024)S(1)} %pad_clamp_fusion), kind=kCustom, calls=%fused_computation.1.clone | custom fusion | bytes 8388672 | tf_op jit(solution)/shard_map/jit(_take)/gather | solution.py:54
  212.7 6.0 %fusion.5 = (bf16[2,16,128,512]{3,2,1,0:T(8,128)(2,1)}, bf16[2,16,128,512]{3,2,1,0:T(8,128)(2,1)}) fusion(bf16[16,2,128,512]{3,2,1,0:T(8,128)(2,1)} %gather_fusion.3, pred[16]{0:T(512)(128)(4,1)S(1)} %compare_and_fusion, bf16[16,2,128,512]{3,2,1,0:T(8,128)(2,1)} %gather_fusion.4), kind=kLoop, calls=%fused_computation.17 | loop fusion | flops 4194304 | bytes 16777232 | tf_op jit(solution)/shard_map/jit(_take)/select_n | solution.py:54
  218.9 1.1 reshape_squeeze.21
  220.1 1.5 copy.42
  221.6 1.7 copy.52
  223.3 2.0 gather_fusion.1
  225.3 0.8 gather_fusion.2
  226.0 1.5 copy_convert_fusion.1
  227.6 1.6 copy_convert_fusion
  229.2 75.5 %all-to-all-done = bf16[32,2,65536]{2,1,0:T(2,128)(2,1)} async-done(((bf16[32,2,65536]{2,1,0:T(2,128)(2,1)}), bf16[32,2,65536]{2,1,0:T(2,128)(2,1)}, u32[]{:S(2)}, u32[]{:S(2)}) %all-to-all-start) | async-done | bytes 8388640 | tf_op jit(solution)/shard_map/all_to_all | solution.py:49
  304.7 26.0 %reshape.125 = bf16[16384,2,2,64]{3,2,1,0:T(2,128)(2,1)} reshape(bf16[32,2,65536]{2,1,0:T(2,128)(2,1)} %all-to-all-done) | data formatting | bytes 16777216
  330.7 36.1 %copy.50 = bf16[2,2,32,64,512]{4,3,2,1,0:T(8,128)(2,1)} copy(bf16[2,2,32,64,512]{3,1,0,4,2:T(2,128)(2,1)} %bitcast.212) | data formatting | bytes 16777216 | tf_op jit(solution)/shard_map/all_to_all | solution.py:49
  366.8 4.0 fusion.55
  372.1 0.7 fusion.16
  372.9 0.8 fusion.26
  373.6 1.4 copy-done.2
  376.5 0.7 fusion.24
  377.2 0.9 copy-done.7
  378.0 0.8 subtract_reduce_fusion.1
  378.9 0.7 copy-done.6
  379.6 0.8 subtract_reduce_fusion
  380.5 74.2 %psum.7 = f32[2,1,2,16,1]{3,2,0,4,1:T(2,128)S(1)} all-reduce(f32[2,1,2,16,1]{3,2,0,4,1:T(2,128)S(1)} %bitcast.230), channel_id=1, replica_groups=mesh['tm'=4,'op'=32] {'op'}, use_global_device_ids=true, to_apply=%region_4.6 | all-reduce | flops 64 | bytes 512 | tf_op jit(solution)/shard_map/psum | solution.py:74
  (39 shorter events, 5.1 us)
Async XLA Ops:
  6.5 50.8 %all-gather.2.cloned.1.call-start = ((), (), s32[]{:S(2)}) async-start(), calls=%async_computation.1 | async-start | bytes 2162688 | tf_op jit(solution)/shard_map/all_gather | solution.py:20
  93.2 6.6 %copy-start.1 = (bf16[2,8192,128]{2,1,0:T(8,128)(2,1)S(1)}, bf16[2,8192,128]{2,1,0:T(8,128)(2,1)}, u32[]{:S(2)}) copy-start(bf16[2,8192,128]{2,1,0:T(8,128)(2,1)} %reshape_squeeze.19) | copy-start | bytes 12582916
  116.7 6.6 %copy-start.4 = (bf16[64,2,16384]{2,0,1:T(8,128)(2,1)S(1)}, bf16[64,2,16384]{2,0,1:T(8,128)(2,1)}, u32[]{:S(2)}) copy-start(bf16[64,2,16384]{2,0,1:T(8,128)(2,1)} %copy.83) | copy-start | bytes 12582916
  190.7 5.4 %copy-start.8 = (s32[16,1]{0,1:T(1,128)S(1)}, s32[16,1]{0,1:T(1,128)}, u32[]{:S(2)}) copy-start(s32[16,1]{0,1:T(1,128)} %param.10) | copy-start | bytes 196
  190.7 114.0 %all-to-all-start = ((bf16[32,2,65536]{2,1,0:T(2,128)(2,1)}), bf16[32,2,65536]{2,1,0:T(2,128)(2,1)}, u32[]{:S(2)}, u32[]{:S(2)}) async-start(bf16[32,2,65536]{2,1,0:T(2,128)(2,1)} %reshape.124), calls=%async_computation | async-start | bytes 16777216 | tf_op jit(solution)/shard_map/all_to_all | solution.py:49
  207.0 5.0 %copy-start = (s32[16,3]{0,1:T(4,128)S(1)}, s32[16,3]{0,1:T(4,128)}, u32[]{:S(2)}) copy-start(s32[16,3]{0,1:T(4,128)} %param.11) | copy-start | bytes 580
  212.7 6.3 %copy-start.5 = (bf16[2,1,1,512,512]{3,4,2,1,0:T(8,128)(2,1)S(1)}, bf16[2,1,1,512,512]{3,4,2,1,0:T(8,128)(2,1)}, u32[]{:S(2)}) copy-start(bf16[2,1,1,512,512]{3,4,2,1,0:T(8,128)(2,1)} %copy.60) | copy-start | bytes 3145732
  366.8 4.7 %copy-start.3 = (bf16[2,16,128,512]{3,2,1,0:T(8,128)(2,1)S(1)}, bf16[2,16,128,512]{3,2,1,0:T(8,128)(2,1)}, u32[]{:S(2)}) copy-start(bf16[2,16,128,512]{3,2,1,0:T(8,128)(2,1)} %get-tuple-element.48) | copy-start | bytes 12582916
  372.8 2.2 copy-start.2
  376.5 1.6 copy-start.7
  378.0 1.6 copy-start.6
Sparse Core Ops, SparseCore 0:
  9.6 47.6 all-gather.1
where the time goes:
time: 467 us; the launch traced here: 462 us
  local copies, waits for them, and re-layouts  212 us (45%)
  waiting for transfers between devices  110 us (24%)
  blocking collectives  74.2 us (16%)
  matrix products  25.6 us (5%)
  between operations  18.1 us (4%)
  other arithmetic  16.8 us (4%)
  starting transfers between devices  5.43 us (1%)
    all_to_all x1, waiting for transfers between devices, on_device(): lax.all_to_all(stacked, 'op', split_axis=3, concat_axis=2, tiled=True)  75.5 us
    psum x1, blocking collectives, on_device(): totals = lax.psum(partial_sum, 'op')  74.2 us
    unnamed x25, local copies, waits for them, and re-layouts  69.1 us
    all_to_all x1, local copies, waits for them, and re-layouts, on_device(): lax.all_to_all(stacked, 'op', split_axis=3, concat_axis=2, tiled=True)  36.1 us
    all_gather x1, waiting for transfers between devices, on_device(): tau_all = lax.all_gather(peram, 'op', axis=3, tiled=True)  34.7 us
    another operation x1, local copies, waits for them, and re-layouts, on_device(): jnp.stack([sink_side(local, t0, p) for local, t0, p in combos], axis=1)  34.5 us
    reshape x4, local copies, waits for them, and re-layouts, sink_side(): y_both = y_both.astype(jnp.bfloat16).reshape(span, 2, NEV * NEV)  27 us
    dot_general x2, matrix products, sink_side(): jnp.einsum('ijck,cjb->ibk', x_both, second, preferred_element_type=jnp.fl...  14.9 us
  transfers between devices with their start and end apart: 2, of which 2 were waited for; matrix products, arithmetic and copies ran while one was open for 9% of the time, Pallas kernels for 0%

commit v1 on v0

--- a/solution.py
+++ b/solution.py
@@ -71,7 +71,7 @@
         per_time.append(jnp.stack([partial_terms[local, t0, 0]], axis=-1))
     per_local = [jnp.stack(per_time, axis=1)]
     partial_sum = jnp.stack(per_local, axis=1)
-    totals = lax.psum(partial_sum, "op")
+    totals = jnp.sum(lax.all_gather(partial_sum, "op"), axis=0)
     return totals * (1.0 / float(NEV**3))
 
 

time: 467 us -> 431 us (0.923)
  blocking collectives: 74.2 us -> 38.8 us
    psum x1 -> x0, blocking collectives: 74.2 us -> none  [on_device(): totals = lax.psum(partial_sum, 'op')]
    all_gather x0 -> x1, blocking collectives: none -> 38.8 us  [on_device(): totals = jnp.sum(lax.all_gather(partial_sum, 'op'), axis=0)]
  transfers between devices with their start and end apart: 2 -> 2, of which waited for: 2 -> 2; matrix products, arithmetic and copies ran while one was open for 9% -> 10% of each run, Pallas kernels for 0% -> 0%
where the time goes in v1:
time: 431 us; the launch traced here: 427 us
  local copies, waits for them, and re-layouts  212 us (49%)
  waiting for transfers between devices  110 us (26%)
  blocking collectives  38.8 us (9%)
  matrix products  25.6 us (6%)
  between operations  18.1 us (4%)
  other arithmetic  16.3 us (4%)
  starting transfers between devices  5.43 us (1%)
    all_to_all x1, waiting for transfers between devices, on_device(): lax.all_to_all(stacked, 'op', split_axis=3, concat_axis=2, tiled=True)  75.5 us
    unnamed x25, local copies, waits for them, and re-layouts  69.1 us
    all_gather x1, blocking collectives, on_device(): totals = jnp.sum(lax.all_gather(partial_sum, 'op'), axis=0)  38.8 us
    all_to_all x1, local copies, waits for them, and re-layouts, on_device(): lax.all_to_all(stacked, 'op', split_axis=3, concat_axis=2, tiled=True)  36.1 us
    all_gather x1, waiting for transfers between devices, on_device(): tau_all = lax.all_gather(peram, 'op', axis=3, tiled=True)  34.7 us
    another operation x1, local copies, waits for them, and re-layouts, on_device(): jnp.stack([sink_side(local, t0, p) for local, t0, p in combos], axis=1)  34.5 us
    reshape x4, local copies, waits for them, and re-layouts, sink_side(): y_both = y_both.astype(jnp.bfloat16).reshape(span, 2, NEV * NEV)  27 us
    dot_general x2, matrix products, sink_side(): jnp.einsum('ijck,cjb->ibk', x_both, second, preferred_element_type=jnp.fl...  14.9 us
  transfers between devices with their start and end apart: 2, of which 2 were waited for; matrix products, arithmetic and copies ran while one was open for 10% of the time, Pallas kernels for 0%

profile of v1, /device:TPU:1, one launch (start us, length us, event | category | flops | bytes accessed | tf_op | source)
XLA Modules:
  0.0 426.8 jit_solution(5722338821308368324)
XLA Ops:
  6.5 1.5 copy.40
  8.1 1.2 constant_dynamic-slice_fusion.1
  11.3 0.8 constant_dynamic-slice_fusion
  15.2 7.4 %reshape_squeeze.19 = bf16[2,8192,128]{2,1,0:T(8,128)(2,1)} reshape(bf16[2,1,64,16384]{3,2,1,0:T(8,128)(2,1)} %param.7) | data formatting | bytes 8388608 | tf_op jit(solution)/shard_map/reshape;squeeze | solution.py:36
  22.6 34.7 %all-gather.3.cloned.1.call-done = bf16[2,1,2,512,512]{4,2,1,0,3:T(2,128)(2,1)} async-done(((bf16[2,1,2,16,512]{4,2,1,0,3:T(2,128)(2,1)}), bf16[2,1,2,512,512]{4,2,1,0,3:T(2,128)(2,1)}) %all-gather.3.cloned.1.call-update) | async-done | bytes 2097168 | tf_op jit(solution)/shard_map/all_gather | solution.py:20
  57.3 6.5 %fusion.58 = (bf16[2,1,1,512,512]{4,2,1,0,3:T(2,128)(2,1)}, bf16[2,1,1,512,512]{4,2,1,0,3:T(2,128)(2,1)S(1)}) fusion(bf16[2,1,2,512,512]{4,2,1,0,3:T(2,128)(2,1)} %all-gather.3.cloned.1.call-done), kind=kLoop, calls=%fused_computation.113 | loop fusion | bytes 4194304 | tf_op jit(solution)/shard_map/slice | solution.py:62
  63.8 4.6 %copy.64 = bf16[2,1,1,512,512]{3,4,2,1,0:T(8,128)(2,1)S(1)} copy(bf16[2,1,1,512,512]{4,2,1,0,3:T(2,128)(2,1)} %get-tuple-element.24) | data formatting | bytes 2097152
  68.4 4.2 copy.65
  72.6 0.8 dynamic-slice_bitcast_fusion.3
  73.4 0.8 fusion.54
  74.2 3.5 fusion.15
  77.7 1.2 copy.66
  78.9 7.4 %fusion.2 = bf16[64,256,128]{2,1,0:T(8,128)(2,1)} fusion(bf16[64,128,2,128]{1,0,3,2:T(8,128)(2,1)S(1)} %bitcast.217, bf16[1,128,256]{1,2,0:T(8,128)(2,1)S(1)} %get-tuple-element.35, bf16[1,128,256]{1,2,0:T(8,128)(2,1)S(1)} %get-tuple-element.34), kind=kOutput, calls=%fused_computation.12 | convolution fusion | flops 1076101120 | bytes 8519680 | tf_op jit(solution)/shard_map/ijck,cjb->ibk/dot_general | solution.py:39
  86.4 6.9 %reshape.86 = bf16[64,2,16384]{2,1,0:T(2,128)(2,1)} reshape(bf16[64,256,128]{2,1,0:T(8,128)(2,1)} %fusion.2) | data formatting | bytes 8388608 | tf_op jit(solution)/shard_map/reshape | solution.py:40
  93.2 6.6 %copy.90 = bf16[64,2,16384]{2,0,1:T(8,128)(2,1)} copy(bf16[64,2,16384]{2,1,0:T(2,128)(2,1)} %reshape.86) | data formatting | bytes 8388608 | tf_op jit(solution)/shard_map/reshape | solution.py:40
  99.9 1.3 fusion.14
  101.2 1.2 copy.67
  102.4 7.4 %fusion.3 = bf16[64,256,128]{2,1,0:T(8,128)(2,1)} fusion(bf16[64,128,2,128]{1,0,3,2:T(8,128)(2,1)S(1)} %bitcast.218, bf16[1,128,256]{1,2,0:T(8,128)(2,1)S(1)} %get-tuple-element.39, bf16[1,128,256]{1,2,0:T(8,128)(2,1)S(1)} %get-tuple-element.38), kind=kOutput, calls=%fused_computation.13 | convolution fusion | flops 1076101120 | bytes 8519680 | tf_op jit(solution)/shard_map/ijck,cjb->ibk/dot_general | solution.py:39
  109.8 6.9 %reshape.88 = bf16[64,2,16384]{2,1,0:T(2,128)(2,1)} reshape(bf16[64,256,128]{2,1,0:T(8,128)(2,1)} %fusion.3) | data formatting | bytes 8388608 | tf_op jit(solution)/shard_map/reshape | solution.py:40
  116.7 6.6 %copy.89 = bf16[64,2,16384]{2,0,1:T(8,128)(2,1)} copy(bf16[64,2,16384]{2,1,0:T(2,128)(2,1)} %reshape.88) | data formatting | bytes 8388608 | tf_op jit(solution)/shard_map/reshape | solution.py:40
  123.3 6.2 %pad_maximum_fusion = bf16[2,2,64,16384]{3,2,1,0:T(8,128)(2,1)} fusion(bf16[2,1,64,16384]{3,2,1,0:T(8,128)(2,1)} %bitcast.221, bf16[2,1,64,16384]{3,2,1,0:T(8,128)(2,1)S(1)} %bitcast.219), kind=kLoop, calls=%fused_computation.9 | loop fusion | flops 4194304 | bytes 16777216 | tf_op jit(solution)/shard_map/stack | solution.py:48
  129.5 34.5 %copy.49 = bf16[2,2,64,16384]{2,1,0,3:T(2,128)(2,1)} copy(bf16[2,2,64,16384]{3,2,1,0:T(8,128)(2,1)} %pad_maximum_fusion) | data formatting | bytes 16777216 | tf_op jit(solution)/shard_map/stack | solution.py:48
  164.0 26.7 %reshape.137 = bf16[32,2,65536]{2,1,0:T(2,128)(2,1)} reshape(bf16[16384,2,2,64]{3,2,1,0:T(2,128)(2,1)} %bitcast.210) | data formatting | bytes 16777216
  190.7 5.4 %all-to-all-start = ((bf16[32,2,65536]{2,1,0:T(2,128)(2,1)}), bf16[32,2,65536]{2,1,0:T(2,128)(2,1)}, u32[]{:S(2)}, u32[]{:S(2)}) async-start(bf16[32,2,65536]{2,1,0:T(2,128)(2,1)} %reshape.137), calls=%async_computation | async-start | bytes 16777216 | tf_op jit(solution)/shard_map/all_to_all | solution.py:49
  196.2 5.8 %fusion.57 = (bf16[2,1,2048,512]{3,2,1,0:T(8,128)(2,1)}, bf16[2,1,2048,512]{3,2,1,0:T(8,128)(2,1)}) fusion(bf16[2,2,2048,512]{3,2,1,0:T(8,128)(2,1)} %param.8), kind=kLoop, calls=%fused_computation.112 | loop fusion | bytes 16777216 | tf_op jit(solution)/shard_map/slice | solution.py:53
  202.0 5.0 %gather_fusion.3 = bf16[16,2,128,512]{3,2,1,0:T(8,128)(2,1)} fusion(bf16[2,16,128,512]{3,2,1,0:T(8,128)(2,1)} %bitcast.222, s32[1024]{0:T(1024)S(1)} %pad_clamp_fusion), kind=kCustom, calls=%fused_computation.clone | custom fusion | bytes 8388672 | tf_op jit(solution)/shard_map/jit(_take)/gather | solution.py:54
  207.0 5.0 %gather_fusion.4 = bf16[16,2,128,512]{3,2,1,0:T(8,128)(2,1)} fusion(bf16[2,16,128,512]{3,2,1,0:T(8,128)(2,1)} %bitcast.220, s32[1024]{0:T(1024)S(1)} %pad_clamp_fusion), kind=kCustom, calls=%fused_computation.1.clone | custom fusion | bytes 8388672 | tf_op jit(solution)/shard_map/jit(_take)/gather | solution.py:54
  212.7 6.0 %fusion.5 = (bf16[2,16,128,512]{3,2,1,0:T(8,128)(2,1)}, bf16[2,16,128,512]{3,2,1,0:T(8,128)(2,1)}) fusion(bf16[16,2,128,512]{3,2,1,0:T(8,128)(2,1)} %gather_fusion.3, pred[16]{0:T(512)(128)(4,1)S(1)} %compare_and_fusion, bf16[16,2,128,512]{3,2,1,0:T(8,128)(2,1)} %gather_fusion.4), kind=kLoop, calls=%fused_computation.17 | loop fusion | flops 4194304 | bytes 16777232 | tf_op jit(solution)/shard_map/jit(_take)/select_n | solution.py:54
  218.9 1.1 reshape_squeeze.21
  220.1 1.5 copy.42
  221.6 1.7 copy.52
  223.3 2.0 gather_fusion.1
  225.3 0.8 gather_fusion.2
  226.0 1.5 copy_convert_fusion.1
  227.6 1.6 copy_convert_fusion
  229.2 75.5 %all-to-all-done = bf16[32,2,65536]{2,1,0:T(2,128)(2,1)} async-done(((bf16[32,2,65536]{2,1,0:T(2,128)(2,1)}), bf16[32,2,65536]{2,1,0:T(2,128)(2,1)}, u32[]{:S(2)}, u32[]{:S(2)}) %all-to-all-start) | async-done | bytes 8388640 | tf_op jit(solution)/shard_map/all_to_all | solution.py:49
  304.7 26.0 %reshape.138 = bf16[16384,2,2,64]{3,2,1,0:T(2,128)(2,1)} reshape(bf16[32,2,65536]{2,1,0:T(2,128)(2,1)} %all-to-all-done) | data formatting | bytes 16777216
  330.7 36.1 %copy.50 = bf16[2,2,32,64,512]{4,3,2,1,0:T(8,128)(2,1)} copy(bf16[2,2,32,64,512]{3,1,0,4,2:T(2,128)(2,1)} %bitcast.211) | data formatting | bytes 16777216 | tf_op jit(solution)/shard_map/all_to_all | solution.py:49
  366.8 4.0 fusion.56
  372.1 0.7 fusion.16
  372.9 0.8 fusion.26
  373.6 1.4 copy-done.2
  376.5 0.7 fusion.24
  377.2 0.9 copy-done.7
  378.0 0.8 subtract_reduce_fusion.1
  378.9 0.7 copy-done.6
  379.6 0.8 subtract_reduce_fusion
  380.5 38.8 %all-gather = f32[64,2,16,1]{2,1,3,0:T(2,128)S(1)} all-gather(f32[2,2,16,1]{2,1,3,0:T(2,128)S(1)} %copy.55), channel_id=2, replica_groups=mesh['tm'=4,'op'=32] {'op'}, dimensions={0}, use_global_device_ids=true | all-gather | bytes 8448 | tf_op jit(solution)/shard_map/all_gather | solution.py:74
  (41 shorter events, 5.2 us)
Async XLA Ops:
  6.5 50.8 %all-gather.3.cloned.1.call-start = ((), (), s32[]{:S(2)}) async-start(), calls=%async_computation.1 | async-start | bytes 2162688 | tf_op jit(solution)/shard_map/all_gather | solution.py:20
  93.2 6.6 %copy-start.1 = (bf16[2,8192,128]{2,1,0:T(8,128)(2,1)S(1)}, bf16[2,8192,128]{2,1,0:T(8,128)(2,1)}, u32[]{:S(2)}) copy-start(bf16[2,8192,128]{2,1,0:T(8,128)(2,1)} %reshape_squeeze.19) | copy-start | bytes 12582916
  116.7 6.6 %copy-start.4 = (bf16[64,2,16384]{2,0,1:T(8,128)(2,1)S(1)}, bf16[64,2,16384]{2,0,1:T(8,128)(2,1)}, u32[]{:S(2)}) copy-start(bf16[64,2,16384]{2,0,1:T(8,128)(2,1)} %copy.90) | copy-start | bytes 12582916
  190.7 5.4 %copy-start.8 = (s32[16,1]{0,1:T(1,128)S(1)}, s32[16,1]{0,1:T(1,128)}, u32[]{:S(2)}) copy-start(s32[16,1]{0,1:T(1,128)} %param.10) | copy-start | bytes 196
  190.7 114.0 %all-to-all-start = ((bf16[32,2,65536]{2,1,0:T(2,128)(2,1)}), bf16[32,2,65536]{2,1,0:T(2,128)(2,1)}, u32[]{:S(2)}, u32[]{:S(2)}) async-start(bf16[32,2,65536]{2,1,0:T(2,128)(2,1)} %reshape.137), calls=%async_computation | async-start | bytes 16777216 | tf_op jit(solution)/shard_map/all_to_all | solution.py:49
  207.0 5.0 %copy-start = (s32[16,3]{0,1:T(4,128)S(1)}, s32[16,3]{0,1:T(4,128)}, u32[]{:S(2)}) copy-start(s32[16,3]{0,1:T(4,128)} %param.11) | copy-start | bytes 580
  212.7 6.3 %copy-start.5 = (bf16[2,1,1,512,512]{3,4,2,1,0:T(8,128)(2,1)S(1)}, bf16[2,1,1,512,512]{3,4,2,1,0:T(8,128)(2,1)}, u32[]{:S(2)}) copy-start(bf16[2,1,1,512,512]{3,4,2,1,0:T(8,128)(2,1)} %copy.65) | copy-start | bytes 3145732
  366.8 4.7 %copy-start.3 = (bf16[2,16,128,512]{3,2,1,0:T(8,128)(2,1)S(1)}, bf16[2,16,128,512]{3,2,1,0:T(8,128)(2,1)}, u32[]{:S(2)}) copy-start(bf16[2,16,128,512]{3,2,1,0:T(8,128)(2,1)} %get-tuple-element.48) | copy-start | bytes 12582916
  372.8 2.2 copy-start.2
  376.5 1.6 copy-start.7
  378.0 1.6 copy-start.6
Sparse Core Ops, SparseCore 0:
  9.6 47.6 all-gather.2
